TPU v7x, 128 devices: a whole 4x4x4 slice. The times are simulated.
128 devices in a mesh: row: 8 (over x_lo, z), col: 16 (over x_hi, y, core).
Axes of the slice: x: 4 (x_hi: 2, x_lo: 2; x = x_hi * 2 + x_lo), y: 4, z: 4, core: 2. Of those that a mesh axis runs over, the one named last changes fastest.
Arguments:
- amplitudes: bfloat16 [8192, 4096], P('row', 'col'), may hold values from -6 to 6
- amp_mask: int32 [64, 32], P('row', 'col'), may hold values 0 or 1
- integrals: bfloat16 [4096, 32768], P('row', 'col'), may hold values from -0.1875 to 0.1875
- int_tiles: int32 [8, 16, 32], P(None, 'col'), may hold values from 0 to 64, as said below
- pair_dest: int32 [8192], P('row'), may hold values from 0 to 15, as said below
Outputs:
- moved: bfloat16 [16384, 32768], P(('row', 'col'))
Inputs may be any that keep to these rules, and one draw needn't show every extreme that they name: `int_tiles`: entry t of a list names the nonzero tile (t // 16, t mod 16) of that integral block; the entries naming tiles are distinct, the value 64 marks an empty entry, and some block has all 32 entries filled. `pair_dest`: within each row block of 1024 consecutive pairs no column index is named by more than 128 pairs, and one is named by exactly 128.
All inputs are finite; a program needn't handle non-finite values. No bound on the sum of `amp_mask` on one device may be relied on, other than what follows from the above.
Results may differ from a plain program's by a relative error of at most 0.001.
Values may be sent and summed in bfloat16 or wider, within the bound.
A program may use at most 128 MiB of HBM per device.

v0:
```python
import jax
import jax.numpy as jnp
from jax import lax
from jax.sharding import PartitionSpec as P

TILE = 128


def on_device(amplitudes, amp_mask, integrals, int_tiles, pair_dest):
    pair_rows, amp_cols = amplitudes.shape
    int_rows, int_cols = integrals.shape
    row_tiles = int_rows // TILE
    col_tiles = int_cols // TILE
    block_tiles = row_tiles * col_tiles
    amp_scale = amp_mask.astype(jnp.bfloat16)
    amp_used = (
        amplitudes.reshape(amp_mask.shape[0], TILE, amp_mask.shape[1], TILE)
        * amp_scale[:, None, :, None]
    ).reshape(pair_rows, amp_cols)
    all_lists = int_tiles[:, 0, :]
    tile_ids = jnp.arange(block_tiles, dtype=jnp.int32)
    own_list = lax.dynamic_index_in_dim(all_lists, lax.axis_index("row"), 0, keepdims=False)
    own_tiles = jnp.any(own_list[:, None] == tile_ids[None, :], axis=0)
    own_scale = own_tiles.reshape(row_tiles, col_tiles).astype(jnp.bfloat16)
    int_used = (
        integrals.reshape(row_tiles, TILE, col_tiles, TILE) * own_scale[:, None, :, None]
    ).reshape(int_rows, int_cols)
    int_panel = lax.all_gather(int_used, "row", axis=0, tiled=True)
    ladder = jnp.dot(
        lax.all_gather(amp_used, "col", axis=1, tiled=True),
        int_panel,
        preferred_element_type=jnp.float32,
    ).astype(jnp.bfloat16)
    col_count = lax.axis_size("col")
    capacity = 2 * pair_rows // col_count
    col_ids = jnp.arange(col_count, dtype=jnp.int32)
    onehot = (pair_dest[:, None] == col_ids[None, :]).astype(jnp.int32)
    before = jnp.cumsum(onehot, axis=0) - onehot
    slot_of = jnp.sum(before * onehot, axis=1)
    outgoing = (
        jnp.zeros((col_count, capacity, int_cols), jnp.bfloat16).at[pair_dest, slot_of].set(ladder)
    )
    arrived = lax.all_to_all(outgoing, "col", split_axis=0, concat_axis=2, tiled=True)
    return arrived.reshape(capacity, col_count * int_cols)


def solution(mesh):
    in_specs = (P("row", "col"), P("row", "col"), P("row", "col"), P(None, "col", None), P("row"))
    out_specs = P(("row", "col"), None)
    return jax.shard_map(
        on_device, mesh=mesh, in_specs=in_specs, out_specs=out_specs, check_vma=False
    )
```

profile of v0, /device:TPU:1, one launch (start us, length us, event | category | flops | bytes accessed | tf_op | source)
XLA Modules:
  0.0 429.8 jit_solution(8214052948781260305)
XLA Ops:
  6.5 0.0 all-gather.3.cloned.1.call-start
  6.6 0.7 convert_element_type.25
  7.3 0.1 copy.19
  7.4 0.3 mul.26
  7.7 2.0 bitcast_multiply_fusion.1
  9.7 0.0 all-gather.5.cloned.1.call-start
  9.8 0.1 fusion.7
  9.9 0.1 reshape.58
  10.0 0.3 mul.29
  10.3 3.4 bitcast_multiply_fusion
  13.8 4.5 %reduce-window.6 = s32[16,8,128]{2,1,0:T(8,128)S(1)} reduce-window(s32[16,8,128]{2,1,0:T(8,128)S(1)} %fusion.6, s32[]{:T(128)} %constant.9.clone.1), window={size=1x1x128 pad=0_0x0_0x127_0}, to_apply=%region_0.1 | reduce-window | flops 2080768 | bytes 131076 | tf_op jit(solution)/shard_map/reduce-window
  18.3 0.1 slice.8
  18.4 0.1 copy.17
  18.5 0.1 copy.18
  18.6 0.1 broadcast_add_fusion
  18.8 0.1 multiply_reduce_fusion
  18.9 0.1 and_reduce_fusion
  19.0 70.8 %all-gather.3.cloned.1.call-done = bf16[1024,4096]{1,0:T(8,128)(2,1)} async-done(((bf16[1024,256]{1,0:T(8,128)(2,1)}), bf16[1024,4096]{1,0:T(8,128)(2,1)}) %all-gather.3.cloned.1.call-update) | async-done | bytes 8388624 | tf_op jit(solution)/shard_map/all_gather | solution.py:30
  89.8 169.3 %all-gather.5.cloned.1.call-done = bf16[4096,2048]{1,0:T(8,128)(2,1)} async-done(((bf16[512,2048]{1,0:T(8,128)(2,1)}), bf16[4096,2048]{1,0:T(8,128)(2,1)}) %all-gather.5.cloned.1.call-update) | async-done | bytes 16777232 | tf_op jit(solution)/shard_map/all_gather | solution.py:28
  259.1 24.0 %fusion.8 = f32[1024,2048]{1,0:T(8,128)} fusion(bf16[1024,4096]{1,0:T(8,128)(2,1)} %all-gather.3.cloned.1.call-done, bf16[4096,2048]{1,0:T(8,128)(2,1)} %all-gather.5.cloned.1.call-done), kind=kOutput, calls=%fused_computation.23 | convolution fusion | flops 17179869184 | bytes 33554432 | tf_op jit(solution)/shard_map/dot_general | solution.py:29
  283.1 12.9 %scatter_custom_fusion = bf16[2048,2048]{1,0:T(8,128)(2,1)} fusion(s32[1024]{0:T(1024)S(1)} %broadcast_select_fusion, bf16[]{:T(256)} %constant.8.clone.1, f32[1024,2048]{1,0:T(8,128)} %fusion.8), kind=kCustom, calls=%fused_computation.1 | custom fusion | flops 2097152 | bytes 16777218
  295.9 102.8 %all_to_all.15 = bf16[16,128,2048]{2,1,0:T(8,128)(2,1)} all-to-all(bf16[16,128,2048]{2,1,0:T(8,128)(2,1)} %bitcast.39), channel_id=1, replica_groups=mesh['row'=8,'col'=16] {'col'}, dimensions={0} | all-to-all | bytes 16777216 | tf_op jit(solution)/shard_map/all_to_all | solution.py:43
  398.7 12.3 %copy.20 = bf16[1,128,16,2048]{1,3,2,0:T(8,128)(2,1)} copy(bf16[1,128,16,2048]{3,1,2,0:T(8,128)(2,1)} %bitcast.40) | data formatting | bytes 16777216 | tf_op jit(solution)/shard_map/all_to_all | solution.py:43
  411.0 11.9 %copy.21 = bf16[128,32768]{1,0:T(8,128)(2,1)} copy(bf16[128,32768]{0,1:T(8,128)(2,1)} %bitcast.41) | data formatting | bytes 16777216 | tf_op jit(solution)/shard_map/reshape | solution.py:44
  (21 shorter events, 0.2 us)
Async XLA Ops:
  6.5 3.2 copy-start
  6.5 12.2 %copy-start.4 = (s32[2]{0:T(128)S(1)}, s32[2]{0:T(128)}, u32[]{:S(2)}) copy-start(s32[2]{0:T(128)} %constant.29) | copy-start | bytes 28
  6.5 12.3 %copy-start.3 = (s32[2]{0:T(128)S(1)}, s32[2]{0:T(128)}, u32[]{:S(2)}) copy-start(s32[2]{0:T(128)} %constant.32) | copy-start | bytes 28
  6.5 7.2 %copy-start.2 = (s32[1024]{0:T(1024)S(1)}, s32[1024]{0:T(1024)}, u32[]{:S(2)}) copy-start(s32[1024]{0:T(1024)} %param.9) | copy-start | bytes 12292
  6.5 83.2 %all-gather.3.cloned.1.call-start = ((), (), s32[]{:S(2)}) async-start(), calls=%async_computation.1 | async-start | bytes 8912896 | tf_op jit(solution)/shard_map/all_gather | solution.py:30
  9.7 249.4 %all-gather.5.cloned.1.call-start = ((), (), s32[]{:S(2)}) async-start(), calls=%async_computation.2 | async-start | bytes 18874368 | tf_op jit(solution)/shard_map/all_gather | solution.py:28
  411.0 11.9 %copy-start.1 = (s32[8,1,32]{2,1,0:T(1,128)S(1)}, s32[8,1,32]{2,1,0:T(1,128)}, u32[]{:S(2)}) copy-start(s32[8,1,32]{2,1,0:T(1,128)} %param.8) | copy-start | bytes 3076
Sparse Core Ops, SparseCore 0:
  9.8 79.8 all-gather.2
  91.4 167.6 all-gather.4
where the time goes:
time: 431 us; the launch traced here: 430 us
  waiting for transfers between devices  240 us (56%)
  blocking collectives  103 us (24%)
  local copies, waits for them, and re-layouts  25.4 us (6%)
  matrix products  24 us (6%)
  other arithmetic  23.9 us (6%)
  between operations  13.5 us (3%)
    all_gather x1, waiting for transfers between devices, on_device(): int_panel = lax.all_gather(int_used, 'row', axis=0, tiled=True)  169 us
    all_to_all x1, blocking collectives, on_device(): lax.all_to_all(outgoing, 'col', split_axis=0, concat_axis=2, tiled=True)  103 us
    all_gather x1, waiting for transfers between devices, on_device(): lax.all_gather(amp_used, 'col', axis=1, tiled=True)  70.8 us
    dot_general x1, matrix products, on_device(): jnp.dot(lax.all_gather(amp_used, 'col', axis=1, tiled=True), int_panel, p...  24 us
    unnamed x4, other arithmetic  13 us
    all_to_all x1, local copies, waits for them, and re-layouts, on_device(): lax.all_to_all(outgoing, 'col', split_axis=0, concat_axis=2, tiled=True)  12.3 us
    reshape x1, local copies, waits for them, and re-layouts, on_device(): return arrived.reshape(capacity, col_count * int_cols)  11.9 us
  transfers between devices with their start and end apart: 2, of which 2 were waited for; matrix products, arithmetic and copies ran while one was open for 2% of the time, Pallas kernels for 0%

commit v1 on v0

v1 whole, which is shorter than its diff:
```python
import functools

import jax
import jax.numpy as jnp
from jax import lax
from jax.experimental import pallas as pl
from jax.experimental.pallas import tpu as pltpu
from jax.sharding import PartitionSpec as P

TILE = 128
MESH = pl.DeviceIdType.MESH
CAP = 128
CHUNK_TILES = 2
CHUNK = CHUNK_TILES * TILE
GROUPS = (16, 8, 8)


def ladder_kernel(
    send_tiles, positions, amp_scale, pair_dest, amp_hbm, int_hbm, out,
    amp_in, int_in, panel, comp, dense, select, key, lad, stage,
    load_sem, amp_send, amp_recv, int_send, int_recv, out_send, out_recv, own_sem,
):
    row, col = lax.axis_index("row"), lax.axis_index("col")
    n_cols = lax.axis_size("col")
    n_rows = lax.axis_size("row")
    pair_rows, amp_cols = amp_hbm.shape
    k_tiles, _, int_cols = int_hbm.shape
    n_tiles = int_cols // TILE
    n_chunks = n_tiles // CHUNK_TILES
    half_rows = pair_rows // 2

    core, y, x_hi = lax.rem(col, 2), lax.rem(lax.div(col, 2), 4), lax.div(col, 8)
    z, x_lo = lax.rem(row, 4), lax.div(row, 4)

    def col_at(dx, dy, dc):
        return lax.rem(x_hi + dx, 2) * 8 + lax.rem(y + dy + 4, 4) * 2 + lax.rem(core + dc, 2)

    def row_at(dx, dz):
        return lax.rem(x_lo + dx, 2) * 4 + lax.rem(z + dz + 4, 4)

    load_amp = pltpu.make_async_copy(amp_hbm, amp_in, load_sem.at[0])
    load_amp.start()
    load_ints = [
        pltpu.make_async_copy(
            int_hbm.at[:, :, n * TILE:(n + 1) * TILE], int_in.at[n * k_tiles:(n + 1) * k_tiles], load_sem.at[1 + n]
        )
        for n in range(n_tiles)
    ]
    for load in load_ints:
        load.start()

    barrier = pltpu.get_barrier_semaphore()
    for step in range(1, n_cols):
        peer = lax.rem(col + step, n_cols)
        pl.semaphore_signal(barrier, inc=1, device_id=(row, peer), device_id_type=MESH)
    for dx, dz in ((1, 0), (0, 1), (0, -1)):
        pl.semaphore_signal(barrier, inc=1, device_id=(row_at(dx, dz), col), device_id_type=MESH)

    load_amp.wait()
    own_cols = pl.ds(pl.multiple_of(col * amp_cols, amp_cols), amp_cols)
    for a in range(pair_rows // TILE):
        rows = slice(a * TILE, (a + 1) * TILE)
        panel[rows, own_cols] = amp_in[rows, :] * amp_scale[a:a + 1, :]

    for load in load_ints:
        load.wait()
    first = 0
    for g, count in enumerate(GROUPS):
        for slot in range(count):
            comp[g][row * count + slot] = int_in[send_tiles[first + slot]]
        comp[g][n_rows * count] = jnp.zeros((TILE, TILE), jnp.bfloat16)
        first += count

    pl.semaphore_wait(barrier, n_cols - 1 + 3)

    def amp_piece(owner, half):
        at = pl.ds(pl.multiple_of(owner * amp_cols, amp_cols), amp_cols)
        if half is None:
            return panel.at[:, at]
        return panel.at[half * half_rows:(half + 1) * half_rows, at]

    def amp_copy(sem, owner, half, target):
        piece = amp_piece(owner, half)
        return pltpu.make_async_remote_copy(
            piece, piece, amp_send.at[sem], amp_recv.at[sem], device_id=(row, target), device_id_type=MESH
        )

    def int_piece(g, owner, half):
        count = GROUPS[g]
        if half is None:
            return comp[g].at[pl.ds(owner * count, count)]
        return comp[g].at[pl.ds(owner * count + half * (count // 2), count // 2)]

    def int_copy(sem, g, owner, half, target):
        piece = int_piece(g, owner, half)
        return pltpu.make_async_remote_copy(
            piece, piece, int_send.at[g, sem], int_recv.at[g, sem], device_id=(target, col), device_id_type=MESH
        )

    amp_steps = {
        0: ((0, 0, 0), None, (1, 0, 0), (1, 0, 0)),
        1: ((0, 0, 0), None, (0, 1, 0), (0, -1, 0)),
        2: ((0, 0, 0), None, (0, -1, 0), (0, 1, 0)),
        3: ((1, 0, 0), None, (0, 1, 0), (1, -1, 0)),
        4: ((1, 0, 0), None, (0, -1, 0), (1, 1, 0)),
        5: ((0, -1, 0), 0, (0, 1, 0), (0, 2, 0)),
        6: ((0, 1, 0), 1, (0, -1, 0), (0, 2, 0)),
        7: ((1, -1, 0), 0, (0, 1, 0), (1, 2, 0)),
        8: ((1, 1, 0), 1, (0, -1, 0), (1, 2, 0)),
        9: ((0, 0, 0), None, (0, 0, 1), (0, 0, 1)),
        10: ((0, -1, 0), None, (0, 0, 1), (0, -1, 1)),
        11: ((0, 1, 0), None, (0, 0, 1), (0, 1, 1)),
        12: ((1, 0, 0), None, (0, 0, 1), (1, 0, 1)),
        13: ((1, -1, 0), None, (0, 0, 1), (1, -1, 1)),
        14: ((1, 1, 0), None, (0, 0, 1), (1, 1, 1)),
        15: ((0, 2, 0), None, (0, 0, 1), (0, 2, 1)),
        16: ((1, 2, 0), None, (0, 0, 1), (1, 2, 1)),
    }
    int_steps = {
        0: ((0, 0), None, (1, 0), (1, 0)),
        1: ((0, 0), None, (0, 1), (0, -1)),
        2: ((0, 0), None, (0, -1), (0, 1)),
        3: ((1, 0), None, (0, 1), (1, -1)),
        4: ((1, 0), None, (0, -1), (1, 1)),
        5: ((0, -1), 0, (0, 1), (0, 2)),
        6: ((0, 1), 1, (0, -1), (0, 2)),
        7: ((1, -1), 0, (0, 1), (1, 2)),
        8: ((1, 1), 1, (0, -1), (1, 2)),
    }

    def amp_start(*sems):
        for sem in sems:
            what, half, to, _ = amp_steps[sem]
            amp_copy(sem, col_at(*what), half, col_at(*to)).start()

    def amp_arrived(*sems):
        for sem in sems:
            _, half, to, comes = amp_steps[sem]
            amp_copy(sem, col_at(*comes), half, col_at(*to)).wait_recv()

    def int_start(g, *sems):
        for sem in sems:
            what, half, to, _ = int_steps[sem]
            int_copy(sem, g, row_at(*what), half, row_at(*to)).start()

    def int_arrived(g, *sems):
        for sem in sems:
            _, half, to, comes = int_steps[sem]
            int_copy(sem, g, row_at(*comes), half, row_at(*to)).wait_recv()

    amp_start(0, 1, 2, 9)
    int_start(0, 1, 2, 0)
    for g in range(1, len(GROUPS)):
        int_start(g, 0)

    for block in range(pair_rows // TILE):
        cols = slice(block * TILE, (block + 1) * TILE)
        q = lax.broadcasted_iota(jnp.int32, (pair_rows, TILE), 0)
        p = lax.broadcasted_iota(jnp.int32, (pair_rows, TILE), 1) + block * TILE
        earlier = jnp.where(q < p, 1.0, 0.0).astype(jnp.bfloat16)
        dest_all = lax.broadcasted_iota(jnp.int32, (n_cols, pair_rows), 0)
        onehot = jnp.where(dest_all == pair_dest[...], 1.0, 0.0)
        before = jnp.dot(onehot.astype(jnp.bfloat16), earlier, preferred_element_type=jnp.float32)
        slot = jnp.sum(before * onehot[:, cols], axis=0, keepdims=True)
        key[:, cols] = pair_dest[:, cols] * CAP + slot.astype(jnp.int32)

    def fill_select(d, carry):
        places = lax.broadcasted_iota(jnp.int32, (CAP, pair_rows), 0) + d * CAP
        at = pl.ds(pl.multiple_of(d * CAP, CAP), CAP)
        select[at, :] = jnp.where(places == key[...], 1.0, 0.0).astype(jnp.bfloat16)
        return carry

    lax.fori_loop(0, n_cols, fill_select, 0)

    amp_arrived(1, 2)
    amp_start(5, 6, 10, 11)
    int_arrived(0, 1, 2)
    int_start(0, 5, 6)
    amp_arrived(0)
    amp_start(3, 4, 12)
    int_arrived(0, 0)
    int_start(0, 3, 4)
    amp_arrived(5, 6)
    amp_start(15)
    int_arrived(0, 5, 6)
    amp_arrived(3, 4)
    amp_start(7, 8, 13, 14)
    int_arrived(0, 3, 4)
    int_start(0, 7, 8)
    int_start(1, 1, 2)
    int_arrived(1, 0)
    int_start(1, 3, 4)
    amp_arrived(7, 8)
    amp_start(16)
    amp_arrived(9, 10, 11, 12, 13, 14, 15, 16)
    int_arrived(0, 7, 8)

    def unpack(q, groups):
        def one_row(r, carry):
            for n in range(CHUNK_TILES):
                for k in range(k_tiles):
                    tile = None
                    for g in range(groups):
                        at = positions[((g * n_rows + r) * n_tiles + q * CHUNK_TILES + n) * k_tiles + k]
                        part = comp[g][at]
                        tile = part if tile is None else tile + part
                    down = pl.ds(pl.multiple_of((r * k_tiles + k) * TILE, TILE), TILE)
                    dense[down, n * TILE:(n + 1) * TILE] = tile
            return carry

        lax.fori_loop(0, n_rows, one_row, 0)

    def multiply(q):
        m_rows = pair_rows // 2

        def one_half(m, carry):
            at = pl.ds(pl.multiple_of(m * m_rows, m_rows), m_rows)
            lad[at, :] = jnp.dot(panel[at, :], dense[...], preferred_element_type=jnp.float32).astype(jnp.bfloat16)
            return carry

        lax.fori_loop(0, 2, one_half, 0)
        dests = 4

        def one_part(j, carry):
            at = pl.ds(pl.multiple_of(j * dests * CAP, dests * CAP), dests * CAP)
            rows = jnp.dot(select[at, :], lad[...], preferred_element_type=jnp.float32).astype(jnp.bfloat16)
            stage[q, pl.ds(j * dests, dests)] = rows.reshape(dests, CAP, CHUNK)
            return carry

        lax.fori_loop(0, n_cols // dests, one_part, 0)

    def out_piece(owner, q):
        return out.at[:, pl.ds(pl.multiple_of(owner * int_cols + q * CHUNK, CHUNK), CHUNK)]

    def send(q):
        def one_peer(step, carry):
            peer = lax.rem(col + step, n_cols)
            pltpu.make_async_remote_copy(
                stage.at[q, peer], out_piece(col, q), out_send.at[step], out_recv.at[step],
                device_id=(row, peer), device_id_type=MESH,
            ).start()
            return carry

        lax.fori_loop(1, n_cols, one_peer, 0)
        pltpu.make_async_copy(stage.at[q, col], out_piece(col, q), own_sem.at[q]).start()

    def chunks(lo, hi, groups):
        def one_chunk(q, carry):
            unpack(q, groups)
            multiply(q)
            send(q)
            return carry

        lax.fori_loop(lo, hi, one_chunk, 0)

    chunks(0, 2, 1)
    int_arrived(1, 1, 2)
    int_start(1, 5, 6)
    int_arrived(1, 3, 4)
    int_start(1, 7, 8)
    int_start(2, 1, 2)
    int_arrived(2, 0)
    int_start(2, 3, 4)
    int_arrived(1, 5, 6, 7, 8)
    chunks(2, 3, 2)
    int_arrived(2, 1, 2)
    int_start(2, 5, 6)
    int_arrived(2, 3, 4)
    int_start(2, 7, 8)
    int_arrived(2, 5, 6, 7, 8)
    chunks(3, n_chunks, 3)

    for sem in amp_steps:
        what, half, to, _ = amp_steps[sem]
        amp_copy(sem, col_at(*what), half, col_at(*to)).wait_send()
    for g in range(len(GROUPS)):
        for sem in int_steps:
            what, half, to, _ = int_steps[sem]
            int_copy(sem, g, row_at(*what), half, row_at(*to)).wait_send()

    def own_done(q, carry):
        pltpu.make_async_copy(stage.at[q, col], out_piece(col, q), own_sem.at[q]).wait()
        return carry

    lax.fori_loop(0, n_chunks, own_done, 0)

    def peer_done(step, carry):
        source = lax.rem(col - step + n_cols, n_cols)
        block = out.at[:, pl.ds(pl.multiple_of(source * int_cols, int_cols), int_cols)]
        whole = pltpu.make_async_remote_copy(
            block, block, out_send.at[step], out_recv.at[step], device_id=(row, source), device_id_type=MESH
        )
        whole.wait()
        return carry

    lax.fori_loop(1, n_cols, peer_done, 0)


def copy_kernel(src, dst, buf, in_sem, out_sem):
    parts = buf.shape[0]
    width = src.shape[1] // parts
    reads = [
        pltpu.make_async_copy(src.at[:, i * width:(i + 1) * width], buf.at[i], in_sem.at[i]) for i in range(parts)
    ]
    writes = [
        pltpu.make_async_copy(buf.at[i], dst.at[:, i * width:(i + 1) * width], out_sem.at[i]) for i in range(parts)
    ]
    for read in reads:
        read.start()
    for read, write in zip(reads, writes):
        read.wait()
        write.start()
    for write in writes:
        write.wait()


def on_device(amplitudes, amp_mask, integrals, int_tiles, pair_dest):
    pair_rows, amp_cols = amplitudes.shape
    int_rows, int_cols = integrals.shape
    n_rows, n_cols = lax.axis_size("row"), lax.axis_size("col")
    k_tiles, n_tiles = int_rows // TILE, int_cols // TILE
    block_tiles = k_tiles * n_tiles
    slots = int_tiles.shape[2]
    n_chunks = n_tiles // CHUNK_TILES

    ids = jnp.arange(block_tiles, dtype=jnp.int32)
    tile_of = (ids % k_tiles) * n_tiles + ids // k_tiles
    present = jnp.any(int_tiles[:, 0, :, None] == tile_of[None, None, :], axis=1)
    ahead = present[:, :, None] & (ids[:, None] < ids[None, :])[None]
    rank = jnp.sum(ahead.astype(jnp.int32), axis=1)
    parts, first = [], 0
    for count in GROUPS:
        inside = present & (rank >= first) & (rank < first + count)
        place = jnp.arange(n_rows, dtype=jnp.int32)[:, None] * count + rank - first
        parts.append(jnp.where(inside, place, n_rows * count))
        first += count
    positions = jnp.stack(parts).reshape(-1)
    me = lax.axis_index("row")
    own_present = lax.dynamic_index_in_dim(present, me, 0, keepdims=False)
    own_rank = lax.dynamic_index_in_dim(rank, me, 0, keepdims=False)
    hit = own_present[None, :] & (own_rank[None, :] == jnp.arange(slots, dtype=jnp.int32)[:, None])
    send_tiles = jnp.sum(jnp.where(hit, ids[None, :], 0), axis=1)
    amp_scale = jnp.repeat(amp_mask.astype(jnp.bfloat16), TILE, axis=1)

    any_ref = pl.BlockSpec(memory_space=pl.ANY)
    smem = pl.BlockSpec(memory_space=pltpu.SMEM)
    vmem = pl.BlockSpec(memory_space=pltpu.VMEM)
    spread = pl.pallas_call(
        ladder_kernel,
        out_shape=jax.ShapeDtypeStruct((CAP, n_cols * int_cols), jnp.bfloat16),
        in_specs=[smem, smem, vmem, vmem, any_ref, any_ref],
        out_specs=any_ref,
        scratch_shapes=[
            pltpu.VMEM((pair_rows, amp_cols), jnp.bfloat16),
            pltpu.VMEM((block_tiles, TILE, TILE), jnp.bfloat16),
            pltpu.VMEM((pair_rows, n_cols * amp_cols), jnp.bfloat16),
            [pltpu.VMEM((n_rows * count + 1, TILE, TILE), jnp.bfloat16) for count in GROUPS],
            pltpu.VMEM((n_rows * int_rows, CHUNK), jnp.bfloat16),
            pltpu.VMEM((n_cols * CAP, pair_rows), jnp.bfloat16),
            pltpu.VMEM((1, pair_rows), jnp.int32),
            pltpu.VMEM((pair_rows, CHUNK), jnp.bfloat16),
            pltpu.VMEM((n_chunks, n_cols, CAP, CHUNK), jnp.bfloat16),
            pltpu.SemaphoreType.DMA((1 + n_tiles,)),
            pltpu.SemaphoreType.DMA((17,)),
            pltpu.SemaphoreType.DMA((17,)),
            pltpu.SemaphoreType.DMA((len(GROUPS), 9)),
            pltpu.SemaphoreType.DMA((len(GROUPS), 9)),
            pltpu.SemaphoreType.DMA((n_cols,)),
            pltpu.SemaphoreType.DMA((n_cols,)),
            pltpu.SemaphoreType.DMA((n_chunks,)),
        ],
        name="ladder",
        compiler_params=pltpu.CompilerParams(
            collective_id=0, has_side_effects=True, vmem_limit_bytes=56 * 1024 * 1024
        ),
    )(
        send_tiles, positions, amp_scale, pair_dest.reshape(1, pair_rows), amplitudes,
        integrals.reshape(k_tiles, TILE, int_cols),
    )
    parts_out = 8
    return pl.pallas_call(
        copy_kernel,
        out_shape=jax.ShapeDtypeStruct(spread.shape, spread.dtype),
        in_specs=[any_ref],
        out_specs=any_ref,
        scratch_shapes=[
            pltpu.VMEM((parts_out, CAP, n_cols * int_cols // parts_out), jnp.bfloat16),
            pltpu.SemaphoreType.DMA((parts_out,)),
            pltpu.SemaphoreType.DMA((parts_out,)),
        ],
        name="deliver",
    )(spread)


def solution(mesh):
    in_specs = (P("row", "col"), P("row", "col"), P("row", "col"), P(None, "col", None), P("row"))
    out_specs = P(("row", "col"), None)
    return jax.shard_map(
        on_device, mesh=mesh, in_specs=in_specs, out_specs=out_specs, check_vma=False
    )
```

time: 431 us -> 168 us (0.39)
  waiting for transfers between devices: 240 us -> 0 us
  Pallas kernels: 0 us -> 163 us
  blocking collectives: 103 us -> 0 us
  local copies, waits for them, and re-layouts: 25.4 us -> 1.36 us
  matrix products: 24 us -> 0 us
  other arithmetic: 23.9 us -> 2.37 us
  between operations: 13.5 us -> 0.04 us
    all_gather x2 -> x0, waiting for transfers between devices: 240 us -> none  [the longest x1 169 us: on_device(): int_panel = lax.all_gather(int_used, 'row', axis=0, tiled=True)]
    pallas_call x0 -> x2, Pallas kernels: none -> 163 us  [the longest x1 156 us: on_device(): pl.pallas_call(ladder_kernel, out_shape=jax.ShapeDtypeStruct((CAP, n_cols...]
    all_to_all x1 -> x0, blocking collectives: 103 us -> none  [on_device(): lax.all_to_all(outgoing, 'col', split_axis=0, concat_axis=2, tiled=True)]
    dot_general x1 -> x0, matrix products: 24 us -> none  [on_device(): jnp.dot(lax.all_gather(amp_used, 'col', axis=1, tiled=True), int_panel, p...]
    unnamed x4 -> x0, other arithmetic: 13 us -> none
    all_to_all x1 -> x0, local copies, waits for them, and re-layouts: 12.3 us -> none  [on_device(): lax.all_to_all(outgoing, 'col', split_axis=0, concat_axis=2, tiled=True)]
    reshape x1 -> x2, local copies, waits for them, and re-layouts: 11.9 us -> 1.33 us  [the longest x1 0.67 us: on_device(): positions = jnp.stack(parts).reshape(-1)]
    mul x2 -> x1, other arithmetic: 5.36 us -> 0.01 us  [on_device(): place = jnp.arange(n_rows, dtype=jnp.int32)[:, None] * count + rank - first]
  transfers between devices with their start and end apart: 2 -> 0, of which waited for: 2 -> 0; matrix products, arithmetic and copies ran while one was open for 2% -> 0% of each run, Pallas kernels for 0% -> 0%
where the time goes in v1:
time: 168 us; the launch traced here: 166 us
  Pallas kernels  163 us (97%)
  other arithmetic  2.37 us (1%)
    pallas_call x1, Pallas kernels, on_device(): pl.pallas_call(ladder_kernel, out_shape=jax.ShapeDtypeStruct((CAP, n_cols...  156 us
    pallas_call x1, Pallas kernels, on_device(): pl.pallas_call(copy_kernel, out_shape=jax.ShapeDtypeStruct(spread.shape,...  6.42 us

profile of v1, /device:TPU:1, one launch (start us, length us, event | category | flops | bytes accessed | tf_op | source)
XLA Modules:
  0.0 166.5 jit_solution(2556089100869513131)
XLA Ops:
  0.0 0.7 convert_element_type.7
  0.7 0.8 compare_reduce_fusion
  1.5 0.7 broadcast_bitcast_fusion.amp_scale
  2.2 0.1 convert_reduce_fusion
  2.4 0.6 select_reduce_fusion.send_tiles
  3.0 0.1 add_select_fusion.1
  3.1 0.7 reshape.196.positions
  3.8 156.3 %ladder.1.src = bf16[128,32768]{1,0:T(8,128)(2,1)} custom-call(s32[32]{0:T(128)} %select_reduce_fusion.send_tiles, s32[1536]{0:T(1024)} %reshape.196.positions, bf16[8,256]{1,0:T(8,128)(2,1)} %broadcast_bitcast_fusion.amp_scale, s32[1,1024]{1,0:T(1,128)} %bitcast.53, bf16[1024,256]{1,0:T(8,128)(2,1)} %amp_hbm.1, bf16[4,128,2048]{2,1,0:T(8,128)(2,1)} %bitcast.52), custom_call_target="tpu_custom_call" | custom-call | tf_op jit(solution)/shard_map/ladder/pallas_call | solution.py:348
  160.0 6.4 %deliver.1 = bf16[128,32768]{1,0:T(8,128)(2,1)} custom-call(bf16[128,32768]{1,0:T(8,128)(2,1)} %ladder.1.src), custom_call_target="tpu_custom_call" | custom-call | tf_op jit(solution)/shard_map/deliver/pallas_call | solution.py:381
  (6 shorter events, 0.1 us)

commit v2 on v1

v2 whole, which is shorter than its diff:
```python
import functools

import jax
import jax.numpy as jnp
from jax import lax
from jax.experimental import pallas as pl
from jax.experimental.pallas import tpu as pltpu
from jax.sharding import PartitionSpec as P

TILE = 128
MESH = pl.DeviceIdType.MESH
CAP = 128
CHUNK_TILES = 2
CHUNK = CHUNK_TILES * TILE
GROUPS = (8, 8, 8, 8)
PART = 4

AMP_STEPS = {
    "x0": ((0, 0, 0), 0, (1, 0, 0)),
    "x1": ((0, 0, 0), 1, (1, 0, 0)),
    "p0": ((0, 0, 0), 0, (0, 1, 0)),
    "p1": ((0, 0, 0), 1, (0, 1, 0)),
    "m0": ((0, 0, 0), 0, (0, -1, 0)),
    "m1": ((0, 0, 0), 1, (0, -1, 0)),
    "pp": ((0, -1, 0), 0, (0, 1, 0)),
    "mm": ((0, 1, 0), 1, (0, -1, 0)),
    "xp0": ((1, 0, 0), 0, (0, 1, 0)),
    "xp1": ((1, 0, 0), 1, (0, 1, 0)),
    "xm0": ((1, 0, 0), 0, (0, -1, 0)),
    "xm1": ((1, 0, 0), 1, (0, -1, 0)),
    "xpp": ((1, -1, 0), 0, (0, 1, 0)),
    "xmm": ((1, 1, 0), 1, (0, -1, 0)),
    "c": ((0, 0, 0), None, (0, 0, 1)),
    "cp": ((0, -1, 0), None, (0, 0, 1)),
    "cm": ((0, 1, 0), None, (0, 0, 1)),
    "cq0": ((0, 2, 0), 0, (0, 0, 1)),
    "cq1": ((0, 2, 0), 1, (0, 0, 1)),
    "cx": ((1, 0, 0), None, (0, 0, 1)),
    "cxp": ((1, -1, 0), None, (0, 0, 1)),
    "cxm": ((1, 1, 0), None, (0, 0, 1)),
    "cxq0": ((1, 2, 0), 0, (0, 0, 1)),
    "cxq1": ((1, 2, 0), 1, (0, 0, 1)),
}
INT_STEPS = {
    "x": ((0, 0), None, (1, 0)),
    "p": ((0, 0), None, (0, 1)),
    "m": ((0, 0), None, (0, -1)),
    "pp": ((0, -1), 0, (0, 1)),
    "mm": ((0, 1), 1, (0, -1)),
    "xp": ((1, 0), None, (0, 1)),
    "xm": ((1, 0), None, (0, -1)),
    "xpp": ((1, -1), 0, (0, 1)),
    "xmm": ((1, 1), 1, (0, -1)),
}


def ladder_kernel(
    send_tiles, positions, amp_mask, pair_dest, amp_hbm, int_hbm, out,
    amp_in, int_in, panel, comp, dense, select, key, acc, lad, stage,
    load_sem, amp_send, amp_recv, int_send, int_recv, out_send, out_recv, own_sem,
):
    row, col = lax.axis_index("row"), lax.axis_index("col")
    n_cols = lax.axis_size("col")
    n_rows = lax.axis_size("row")
    pair_rows, amp_cols = amp_hbm.shape
    k_tiles, _, int_cols = int_hbm.shape
    n_tiles = int_cols // TILE
    n_chunks = n_tiles // CHUNK_TILES
    half_rows = pair_rows // 2

    core, y, x_hi = lax.rem(col, 2), lax.rem(lax.div(col, 2), 4), lax.div(col, 8)
    z, x_lo = lax.rem(row, 4), lax.div(row, 4)

    def col_at(dx, dy, dc):
        return lax.rem(x_hi + dx + 2, 2) * 8 + lax.rem(y + dy + 4, 4) * 2 + lax.rem(core + dc + 2, 2)

    def row_at(dx, dz):
        return lax.rem(x_lo + dx + 2, 2) * 4 + lax.rem(z + dz + 4, 4)

    load_amp = pltpu.make_async_copy(amp_hbm, amp_in, load_sem.at[0])
    load_amp.start()
    load_ints = [
        pltpu.make_async_copy(
            int_hbm.at[:, :, n * TILE:(n + 1) * TILE], int_in.at[n * k_tiles:(n + 1) * k_tiles], load_sem.at[1 + n]
        )
        for n in range(n_tiles)
    ]
    for load in load_ints:
        load.start()

    barrier = pltpu.get_barrier_semaphore()
    for step in range(1, n_cols):
        peer = lax.rem(col + step, n_cols)
        pl.semaphore_signal(barrier, inc=1, device_id=(row, peer), device_id_type=MESH)
    for dx, dz in ((1, 0), (0, 1), (0, -1)):
        pl.semaphore_signal(barrier, inc=1, device_id=(row_at(dx, dz), col), device_id_type=MESH)

    def amp_copy(name, seen_by_receiver):
        what, half, to = AMP_STEPS[name]
        sem = list(AMP_STEPS).index(name)
        owner = col_at(*(w - t for w, t in zip(what, to))) if seen_by_receiver else col_at(*what)
        at = pl.ds(pl.multiple_of(owner * amp_cols, amp_cols), amp_cols)
        piece = panel.at[:, at] if half is None else panel.at[half * half_rows:(half + 1) * half_rows, at]
        return pltpu.make_async_remote_copy(
            piece, piece, amp_send.at[sem], amp_recv.at[sem], device_id=(row, col_at(*to)), device_id_type=MESH
        )

    def int_copy(g, name, seen_by_receiver):
        what, half, to = INT_STEPS[name]
        sem = list(INT_STEPS).index(name)
        owner = row_at(*(w - t for w, t in zip(what, to))) if seen_by_receiver else row_at(*what)
        count = GROUPS[g]
        if half is None:
            piece = comp[g].at[pl.ds(owner * count, count)]
        else:
            piece = comp[g].at[pl.ds(owner * count + half * (count // 2), count // 2)]
        return pltpu.make_async_remote_copy(
            piece, piece, int_send.at[g, sem], int_recv.at[g, sem], device_id=(row_at(*to), col), device_id_type=MESH
        )

    def amp_start(*names):
        for name in names:
            amp_copy(name, False).start()

    def amp_arrived(*names):
        for name in names:
            amp_copy(name, True).wait_recv()

    def int_start(g, *names):
        for name in names:
            int_copy(g, name, False).start()

    def int_arrived(g, *names):
        for name in names:
            int_copy(g, name, True).wait_recv()

    load_amp.wait()
    own_cols = pl.multiple_of(col * amp_cols, amp_cols)
    kept = amp_mask[...].astype(jnp.float32).astype(jnp.bfloat16)
    for a in range(pair_rows // TILE):
        for k in range(amp_cols // TILE):
            tile = amp_in[a * TILE:(a + 1) * TILE, k * TILE:(k + 1) * TILE]
            panel[a * TILE:(a + 1) * TILE, pl.ds(own_cols + k * TILE, TILE)] = tile * kept[a:a + 1, k:k + 1]
    pl.semaphore_wait(barrier, n_cols - 1 + 3)
    amp_start("x0", "p0", "m1", "x1", "p1", "m0", "c")

    for load in load_ints:
        load.wait()
    first = 0
    for g, count in enumerate(GROUPS):
        for slot in range(count):
            comp[g][row * count + slot] = int_in[send_tiles[first + slot]]
        comp[g][n_rows * count] = jnp.zeros((TILE, TILE), jnp.bfloat16)
        first += count
    int_start(0, "x", "p", "m")
    int_start(1, "p", "m")

    dest_all = lax.broadcasted_iota(jnp.int32, (n_cols, pair_rows), 0)
    onehot = jnp.where(dest_all == pair_dest[...], 1.0, 0.0)
    for block in range(pair_rows // TILE):
        cols = slice(block * TILE, (block + 1) * TILE)
        q = lax.broadcasted_iota(jnp.int32, (pair_rows, TILE), 0)
        p = lax.broadcasted_iota(jnp.int32, (pair_rows, TILE), 1) + block * TILE
        earlier = jnp.where(q < p, 1.0, 0.0).astype(jnp.bfloat16)
        before = jnp.dot(onehot.astype(jnp.bfloat16), earlier, preferred_element_type=jnp.float32)
        slot = jnp.sum(before * onehot[:, cols], axis=0, keepdims=True)
        ahead = pair_dest[:, cols] - col
        key[:, cols] = jnp.where(ahead < 0, ahead + n_cols, ahead) * CAP + slot.astype(jnp.int32)

    def fill_select(d, carry):
        places = lax.broadcasted_iota(jnp.int32, (CAP, pair_rows), 0) + d * CAP
        at = pl.ds(pl.multiple_of(d * CAP, CAP), CAP)
        select[at, :] = jnp.where(places == key[...], 1.0, 0.0).astype(jnp.bfloat16)
        return carry

    lax.fori_loop(0, n_cols, fill_select, 0)

    def unpack(q, groups):
        def one_row(r, carry):
            for n in range(CHUNK_TILES):
                for k in range(k_tiles):
                    tile = None
                    for g in range(groups):
                        at = positions[((g * n_rows + r) * n_tiles + q * CHUNK_TILES + n) * k_tiles + k]
                        part = comp[g][at]
                        tile = part if tile is None else tile + part
                    down = pl.ds(pl.multiple_of((r * k_tiles + k) * TILE, TILE), TILE)
                    dense[down, n * TILE:(n + 1) * TILE] = tile
            return carry

        lax.fori_loop(0, n_rows, one_row, 0)

    def multiply(start, depth, first, last):
        m_rows = pair_rows // 2

        def one_half(m, carry):
            at = pl.ds(pl.multiple_of(m * m_rows, m_rows), m_rows)
            deep = pl.ds(pl.multiple_of(start, 512), depth)
            total = jnp.dot(panel[at, deep], dense[deep, :], preferred_element_type=jnp.float32)
            if not first:
                total = total + acc[at, :]
            if last:
                lad[at, :] = total.astype(jnp.bfloat16)
            else:
                acc[at, :] = total
            return carry

        lax.fori_loop(0, 2, one_half, 0)

    def out_piece(owner, q):
        return out.at[:, pl.ds(pl.multiple_of(owner * int_cols + q * CHUNK, CHUNK), CHUNK)]

    def send_part(q, j):
        for i in range(PART):
            step = j * PART + i
            peer = lax.rem(col + step, n_cols)

            def to_peer():
                pltpu.make_async_remote_copy(
                    stage.at[q, step], out_piece(col, q), out_send.at[step], out_recv.at[step],
                    device_id=(row, peer), device_id_type=MESH,
                ).start()

            if step == 0:
                pltpu.make_async_copy(stage.at[q, 0], out_piece(col, q), own_sem.at[q]).start()
            else:
                to_peer()

    n_parts = n_cols // PART

    def spread(q):
        for j in range(n_parts):
            at = slice(j * PART * CAP, (j + 1) * PART * CAP)
            rows = jnp.dot(select[at, :], lad[...], preferred_element_type=jnp.float32).astype(jnp.bfloat16)
            stage[q, j * PART:(j + 1) * PART] = rows.reshape(PART, CAP, CHUNK)
            if j > 0:
                send_part(q, j - 1)

    def chunks(lo, hi, groups):
        def one_chunk(q, carry):
            unpack(q, groups)
            send_part(q - 1, n_parts - 1)
            multiply(0, n_cols * amp_cols, True, True)
            spread(q)
            return carry

        lax.fori_loop(lo, hi, one_chunk, 0)

    amp_arrived("p0", "m1")
    amp_start("pp", "mm")
    int_arrived(0, "p", "m")
    int_start(0, "pp", "mm")
    amp_arrived("x0", "x1")
    amp_start("xp0", "xm1", "xp1", "xm0", "cx")
    int_start(1, "x")
    amp_arrived("p1", "m0")
    amp_start("cp", "cm")
    int_arrived(1, "p", "m")
    int_start(1, "pp", "mm")
    amp_arrived("pp", "mm")
    amp_start("cq0", "cq1")
    int_arrived(0, "x")
    int_start(0, "xp", "xm")
    int_start(2, "x")
    amp_arrived("xp0", "xm1")
    amp_start("xpp", "xmm")
    int_arrived(0, "xp", "xm")
    int_start(0, "xpp", "xmm")
    int_start(3, "x")
    int_arrived(1, "x")
    int_start(1, "xp", "xm")
    int_start(2, "p", "m")
    amp_arrived("c", "cp", "cm", "cq0", "cq1")
    amp_arrived("xp1", "xm0")
    amp_start("cxp", "cxm")
    int_arrived(0, "pp", "mm", "xpp", "xmm")

    y_cols = 2 * amp_cols
    x_cols = 4 * y_cols
    far = lax.rem(x_hi + 1, 2) * x_cols
    unpack(0, 1)
    multiply(x_hi * x_cols, x_cols, True, False)
    amp_arrived("cx")
    multiply(far + y * y_cols, y_cols, False, False)
    amp_arrived("xpp")
    amp_start("cxq0")
    amp_arrived("xmm")
    amp_start("cxq1")
    int_arrived(1, "xp", "xm")
    int_start(1, "xpp", "xmm")
    amp_arrived("cxp")
    multiply(far + lax.rem(y + 3, 4) * y_cols, y_cols, False, False)
    amp_arrived("cxm")
    multiply(far + lax.rem(y + 1, 4) * y_cols, y_cols, False, False)
    amp_arrived("cxq0", "cxq1")
    multiply(far + lax.rem(y + 2, 4) * y_cols, y_cols, False, True)
    spread(0)

    int_arrived(2, "x")
    int_start(2, "xp", "xm")
    int_arrived(2, "p", "m")
    int_start(2, "pp", "mm")
    int_start(3, "p", "m")
    int_arrived(1, "pp", "mm", "xpp", "xmm")
    chunks(1, 2, 2)
    int_arrived(2, "xp", "xm")
    int_start(2, "xpp", "xmm")
    int_arrived(3, "x")
    int_start(3, "xp", "xm")
    int_arrived(3, "p", "m")
    int_start(3, "pp", "mm")
    int_arrived(2, "pp", "mm", "xpp", "xmm")
    chunks(2, 3, 3)
    int_arrived(3, "xp", "xm")
    int_start(3, "xpp", "xmm")
    int_arrived(3, "pp", "mm", "xpp", "xmm")
    chunks(3, n_chunks, 4)

    for name in AMP_STEPS:
        amp_copy(name, False).wait_send()
    send_part(n_chunks - 1, n_parts - 1)
    for g in range(len(GROUPS)):
        for name in INT_STEPS:
            int_copy(g, name, False).wait_send()

    def own_done(q, carry):
        pltpu.make_async_copy(stage.at[q, 0], out_piece(col, q), own_sem.at[q]).wait()
        return carry

    lax.fori_loop(0, n_chunks, own_done, 0)

    def peer_done(step, carry):
        source = lax.rem(col - step + n_cols, n_cols)
        block = out.at[:, pl.ds(pl.multiple_of(source * int_cols, int_cols), int_cols)]
        whole = pltpu.make_async_remote_copy(
            block, block, out_send.at[step], out_recv.at[step], device_id=(row, source), device_id_type=MESH
        )
        whole.wait()
        return carry

    lax.fori_loop(1, n_cols, peer_done, 0)


def copy_kernel(src, dst, buf, in_sem, out_sem):
    parts = buf.shape[0]
    width = src.shape[1] // parts
    reads = [
        pltpu.make_async_copy(src.at[:, i * width:(i + 1) * width], buf.at[i], in_sem.at[i]) for i in range(parts)
    ]
    writes = [
        pltpu.make_async_copy(buf.at[i], dst.at[:, i * width:(i + 1) * width], out_sem.at[i]) for i in range(parts)
    ]
    for read in reads:
        read.start()
    for read, write in zip(reads, writes):
        read.wait()
        write.start()
    for write in writes:
        write.wait()


def on_device(amplitudes, amp_mask, integrals, int_tiles, pair_dest):
    pair_rows, amp_cols = amplitudes.shape
    int_rows, int_cols = integrals.shape
    n_rows, n_cols = lax.axis_size("row"), lax.axis_size("col")
    k_tiles, n_tiles = int_rows // TILE, int_cols // TILE
    block_tiles = k_tiles * n_tiles
    slots = int_tiles.shape[2]
    n_chunks = n_tiles // CHUNK_TILES

    ids = jnp.arange(block_tiles, dtype=jnp.int32)
    tile_of = (ids % k_tiles) * n_tiles + ids // k_tiles
    present = jnp.any(int_tiles[:, 0, :, None] == tile_of[None, None, :], axis=1)
    ahead = present[:, :, None] & (ids[:, None] < ids[None, :])[None]
    rank = jnp.sum(ahead.astype(jnp.int32), axis=1)
    parts, first = [], 0
    for count in GROUPS:
        inside = present & (rank >= first) & (rank < first + count)
        place = jnp.arange(n_rows, dtype=jnp.int32)[:, None] * count + rank - first
        parts.append(jnp.where(inside, place, n_rows * count))
        first += count
    positions = jnp.stack(parts).reshape(-1)
    me = lax.axis_index("row")
    own_present = lax.dynamic_index_in_dim(present, me, 0, keepdims=False)
    own_rank = lax.dynamic_index_in_dim(rank, me, 0, keepdims=False)
    hit = own_present[None, :] & (own_rank[None, :] == jnp.arange(slots, dtype=jnp.int32)[:, None])
    send_tiles = jnp.sum(jnp.where(hit, ids[None, :], 0), axis=1)

    any_ref = pl.BlockSpec(memory_space=pl.ANY)
    smem = pl.BlockSpec(memory_space=pltpu.SMEM)
    vmem = pl.BlockSpec(memory_space=pltpu.VMEM)
    spread = pl.pallas_call(
        ladder_kernel,
        out_shape=jax.ShapeDtypeStruct((CAP, n_cols * int_cols), jnp.bfloat16),
        in_specs=[smem, smem, vmem, vmem, any_ref, any_ref],
        out_specs=any_ref,
        scratch_shapes=[
            pltpu.VMEM((pair_rows, amp_cols), jnp.bfloat16),
            pltpu.VMEM((block_tiles, TILE, TILE), jnp.bfloat16),
            pltpu.VMEM((pair_rows, n_cols * amp_cols), jnp.bfloat16),
            [pltpu.VMEM((n_rows * count + 1, TILE, TILE), jnp.bfloat16) for count in GROUPS],
            pltpu.VMEM((n_rows * int_rows, CHUNK), jnp.bfloat16),
            pltpu.VMEM((n_cols * CAP, pair_rows), jnp.bfloat16),
            pltpu.VMEM((1, pair_rows), jnp.int32),
            pltpu.VMEM((pair_rows, CHUNK), jnp.float32),
            pltpu.VMEM((pair_rows, CHUNK), jnp.bfloat16),
            pltpu.VMEM((n_chunks, n_cols, CAP, CHUNK), jnp.bfloat16),
            pltpu.SemaphoreType.DMA((1 + n_tiles,)),
            pltpu.SemaphoreType.DMA((len(AMP_STEPS),)),
            pltpu.SemaphoreType.DMA((len(AMP_STEPS),)),
            pltpu.SemaphoreType.DMA((len(GROUPS), len(INT_STEPS))),
            pltpu.SemaphoreType.DMA((len(GROUPS), len(INT_STEPS))),
            pltpu.SemaphoreType.DMA((n_cols,)),
            pltpu.SemaphoreType.DMA((n_cols,)),
            pltpu.SemaphoreType.DMA((n_chunks,)),
        ],
        name="ladder",
        compiler_params=pltpu.CompilerParams(
            collective_id=0, has_side_effects=True, vmem_limit_bytes=56 * 1024 * 1024
        ),
    )(
        send_tiles, positions, amp_mask, pair_dest.reshape(1, pair_rows), amplitudes,
        integrals.reshape(k_tiles, TILE, int_cols),
    )
    parts_out = 8
    return pl.pallas_call(
        copy_kernel,
        out_shape=jax.ShapeDtypeStruct(spread.shape, spread.dtype),
        in_specs=[any_ref],
        out_specs=any_ref,
        scratch_shapes=[
            pltpu.VMEM((parts_out, CAP, n_cols * int_cols // parts_out), jnp.bfloat16),
            pltpu.SemaphoreType.DMA((parts_out,)),
            pltpu.SemaphoreType.DMA((parts_out,)),
        ],
        name="deliver",
    )(spread)


def solution(mesh):
    in_specs = (P("row", "col"), P("row", "col"), P("row", "col"), P(None, "col", None), P("row"))
    out_specs = P(("row", "col"), None)
    return jax.shard_map(
        on_device, mesh=mesh, in_specs=in_specs, out_specs=out_specs, check_vma=False
    )
```

time: 168 us -> 163 us (0.970)
  Pallas kernels: 163 us -> 157 us
    pallas_call x1, Pallas kernels: 156 us -> 151 us  [on_device(): pl.pallas_call(ladder_kernel, out_shape=jax.ShapeDtypeStruct((CAP, n_cols...]
where the time goes in v2:
time: 163 us; the launch traced here: 161 us
  Pallas kernels  157 us (96%)
  local copies, waits for them, and re-layouts  2.04 us (1%)
  other arithmetic  1.69 us (1%)
    pallas_call x1, Pallas kernels, on_device(): pl.pallas_call(ladder_kernel, out_shape=jax.ShapeDtypeStruct((CAP, n_cols...  151 us
    pallas_call x1, Pallas kernels, on_device(): pl.pallas_call(copy_kernel, out_shape=jax.ShapeDtypeStruct(spread.shape,...  6.42 us

profile of v2, /device:TPU:1, one launch (start us, length us, event | category | flops | bytes accessed | tf_op | source)
XLA Modules:
  0.0 161.1 jit_solution(1679401409885268428)
XLA Ops:
  0.0 0.8 compare_reduce_fusion
  0.8 1.3 copy.7.amp_mask
  2.2 0.1 convert_reduce_fusion
  2.4 0.6 select_reduce_fusion.send_tiles
  3.0 0.1 fusion.3
  3.1 0.7 reshape.230.positions
  3.8 150.9 %ladder.1.src = bf16[128,32768]{1,0:T(8,128)(2,1)} custom-call(s32[32]{0:T(128)} %select_reduce_fusion.send_tiles, s32[2048]{0:T(1024)} %reshape.230.positions, s32[8,2]{1,0:T(8,128)} %copy.7.amp_mask, s32[1,1024]{1,0:T(1,128)} %bitcast.63, bf16[1024,256]{1,0:T(8,128)(2,1)} %amp_hbm.1, bf16[4,128,2048]{2,1,0:T(8,128)(2,1)} %bitcast.62), custom_call_target="tpu_custom_call" | custom-call | tf_op jit(solution)/shard_map/ladder/pallas_call | solution.py:392
  154.7 6.4 %deliver.1 = bf16[128,32768]{1,0:T(8,128)(2,1)} custom-call(bf16[128,32768]{1,0:T(8,128)(2,1)} %ladder.1.src), custom_call_target="tpu_custom_call" | custom-call | tf_op jit(solution)/shard_map/deliver/pallas_call | solution.py:426
  (6 shorter events, 0.0 us)

commit v3 on v2

--- a/solution.py
+++ b/solution.py
@@ -55,9 +55,9 @@
 
 
 def ladder_kernel(
-    send_tiles, positions, amp_mask, pair_dest, amp_hbm, int_hbm, out,
-    amp_in, int_in, panel, comp, dense, select, key, acc, lad, stage,
-    load_sem, amp_send, amp_recv, int_send, int_recv, out_send, out_recv, own_sem,
+    int_tiles, amp_mask, pair_dest, amp_hbm, int_hbm, out,
+    amp_in, int_in, table_in, table, panel, comp, dense, select, key, acc, lad, stage,
+    load_sem, table_sem, amp_send, amp_recv, int_send, int_recv, out_send, out_recv, own_sem,
 ):
     row, col = lax.axis_index("row"), lax.axis_index("col")
     n_cols = lax.axis_size("col")
@@ -94,6 +94,40 @@
         pl.semaphore_signal(barrier, inc=1, device_id=(row, peer), device_id_type=MESH)
     for dx, dz in ((1, 0), (0, 1), (0, -1)):
         pl.semaphore_signal(barrier, inc=1, device_id=(row_at(dx, dz), col), device_id_type=MESH)
+
+    block_tiles = k_tiles * n_tiles
+    slots = int_tiles.shape[1]
+    lane = lax.broadcasted_iota(jnp.int32, (n_rows, TILE), 1)
+    owner_row = lax.broadcasted_iota(jnp.int32, (n_rows, TILE), 0)
+    tile_of = jnp.where(lane < block_tiles, lax.rem(lane, k_tiles) * n_tiles + lax.div(lane, k_tiles), -1)
+    present = jnp.zeros((n_rows, TILE), jnp.int32)
+    for r in range(n_rows):
+        for s in range(slots):
+            present = jnp.where((owner_row == r) & (tile_of == int_tiles[r, s]), 1, present)
+    before_lane = lax.broadcasted_iota(jnp.int32, (TILE, TILE), 0) < lax.broadcasted_iota(jnp.int32, (TILE, TILE), 1)
+    rank = jnp.dot(
+        present.astype(jnp.float32).astype(jnp.bfloat16),
+        jnp.where(before_lane, 1.0, 0.0).astype(jnp.bfloat16),
+        preferred_element_type=jnp.float32,
+    ).astype(jnp.int32)
+    first = 0
+    for g, count in enumerate(GROUPS):
+        inside = (present == 1) & (rank >= first) & (rank < first + count)
+        place = jnp.where(inside, owner_row * count + rank - first, n_rows * count)
+        table_in[g * n_rows:(g + 1) * n_rows, :] = jnp.clip(place, 0, n_rows * count)
+        first += count
+    own_place = jnp.sum(
+        jnp.where((owner_row == row) & (present == 1), rank + 1, 0).astype(jnp.float32), axis=0, keepdims=True
+    )
+    slot_at = lax.broadcasted_iota(jnp.int32, (slots, TILE), 0).astype(jnp.float32) + 1.0
+    tile_at = lax.broadcasted_iota(jnp.int32, (slots, TILE), 1).astype(jnp.float32)
+    own_tile = jnp.sum(jnp.where(own_place == slot_at, tile_at, 0.0), axis=1, keepdims=True)
+    own_first = len(GROUPS) * n_rows
+    table_in[own_first:own_first + slots, :] = jnp.clip(
+        jnp.broadcast_to(own_tile, (slots, TILE)).astype(jnp.int32), 0, block_tiles - 1
+    )
+    load_table = pltpu.make_async_copy(table_in, table, table_sem)
+    load_table.start()
 
     def amp_copy(name, seen_by_receiver):
         what, half, to = AMP_STEPS[name]
@@ -140,16 +174,17 @@
     for a in range(pair_rows // TILE):
         for k in range(amp_cols // TILE):
             tile = amp_in[a * TILE:(a + 1) * TILE, k * TILE:(k + 1) * TILE]
-            panel[a * TILE:(a + 1) * TILE, pl.ds(own_cols + k * TILE, TILE)] = tile * kept[a:a + 1, k:k + 1]
+            panel[a * TILE:(a + 1) * TILE, pl.ds(own_cols + k * TILE, TILE)] = tile * kept[k:k + 1, a:a + 1]
     pl.semaphore_wait(barrier, n_cols - 1 + 3)
     amp_start("x0", "p0", "m1", "x1", "p1", "m0", "c")
 
+    load_table.wait()
     for load in load_ints:
         load.wait()
     first = 0
     for g, count in enumerate(GROUPS):
         for slot in range(count):
-            comp[g][row * count + slot] = int_in[send_tiles[first + slot]]
+            comp[g][row * count + slot] = int_in[table[own_first + first + slot, 0]]
         comp[g][n_rows * count] = jnp.zeros((TILE, TILE), jnp.bfloat16)
         first += count
     int_start(0, "x", "p", "m")
@@ -181,7 +216,7 @@
                 for k in range(k_tiles):
                     tile = None
                     for g in range(groups):
-                        at = positions[((g * n_rows + r) * n_tiles + q * CHUNK_TILES + n) * k_tiles + k]
+                        at = table[g * n_rows + r, (q * CHUNK_TILES + n) * k_tiles + k]
                         part = comp[g][at]
                         tile = part if tile is None else tile + part
                     down = pl.ds(pl.multiple_of((r * k_tiles + k) * TILE, TILE), TILE)
@@ -341,19 +376,13 @@
     lax.fori_loop(1, n_cols, peer_done, 0)
 
 
-def copy_kernel(src, dst, buf, in_sem, out_sem):
-    parts = buf.shape[0]
-    width = src.shape[1] // parts
-    reads = [
-        pltpu.make_async_copy(src.at[:, i * width:(i + 1) * width], buf.at[i], in_sem.at[i]) for i in range(parts)
+def copy_kernel(src, dst, sem):
+    rows = TILE // sem.shape[0]
+    writes = [
+        pltpu.make_async_copy(src.at[i * rows:(i + 1) * rows], dst.at[i * rows:(i + 1) * rows], sem.at[i])
+        for i in range(sem.shape[0])
     ]
-    writes = [
-        pltpu.make_async_copy(buf.at[i], dst.at[:, i * width:(i + 1) * width], out_sem.at[i]) for i in range(parts)
-    ]
-    for read in reads:
-        read.start()
-    for read, write in zip(reads, writes):
-        read.wait()
+    for write in writes:
         write.start()
     for write in writes:
         write.wait()
@@ -368,35 +397,20 @@
     slots = int_tiles.shape[2]
     n_chunks = n_tiles // CHUNK_TILES
 
-    ids = jnp.arange(block_tiles, dtype=jnp.int32)
-    tile_of = (ids % k_tiles) * n_tiles + ids // k_tiles
-    present = jnp.any(int_tiles[:, 0, :, None] == tile_of[None, None, :], axis=1)
-    ahead = present[:, :, None] & (ids[:, None] < ids[None, :])[None]
-    rank = jnp.sum(ahead.astype(jnp.int32), axis=1)
-    parts, first = [], 0
-    for count in GROUPS:
-        inside = present & (rank >= first) & (rank < first + count)
-        place = jnp.arange(n_rows, dtype=jnp.int32)[:, None] * count + rank - first
-        parts.append(jnp.where(inside, place, n_rows * count))
-        first += count
-    positions = jnp.stack(parts).reshape(-1)
-    me = lax.axis_index("row")
-    own_present = lax.dynamic_index_in_dim(present, me, 0, keepdims=False)
-    own_rank = lax.dynamic_index_in_dim(rank, me, 0, keepdims=False)
-    hit = own_present[None, :] & (own_rank[None, :] == jnp.arange(slots, dtype=jnp.int32)[:, None])
-    send_tiles = jnp.sum(jnp.where(hit, ids[None, :], 0), axis=1)
-
     any_ref = pl.BlockSpec(memory_space=pl.ANY)
+    hbm = pl.BlockSpec(memory_space=pltpu.HBM)
     smem = pl.BlockSpec(memory_space=pltpu.SMEM)
     vmem = pl.BlockSpec(memory_space=pltpu.VMEM)
     spread = pl.pallas_call(
         ladder_kernel,
-        out_shape=jax.ShapeDtypeStruct((CAP, n_cols * int_cols), jnp.bfloat16),
-        in_specs=[smem, smem, vmem, vmem, any_ref, any_ref],
-        out_specs=any_ref,
+        out_shape=pltpu.VMEM((CAP, n_cols * int_cols), jnp.bfloat16),
+        in_specs=[smem, vmem, vmem, hbm, hbm],
+        out_specs=vmem,
         scratch_shapes=[
             pltpu.VMEM((pair_rows, amp_cols), jnp.bfloat16),
             pltpu.VMEM((block_tiles, TILE, TILE), jnp.bfloat16),
+            pltpu.VMEM((len(GROUPS) * n_rows + slots, TILE), jnp.int32),
+            pltpu.SMEM((len(GROUPS) * n_rows + slots, TILE), jnp.int32),
             pltpu.VMEM((pair_rows, n_cols * amp_cols), jnp.bfloat16),
             [pltpu.VMEM((n_rows * count + 1, TILE, TILE), jnp.bfloat16) for count in GROUPS],
             pltpu.VMEM((n_rows * int_rows, CHUNK), jnp.bfloat16),
@@ -406,6 +420,7 @@
             pltpu.VMEM((pair_rows, CHUNK), jnp.bfloat16),
             pltpu.VMEM((n_chunks, n_cols, CAP, CHUNK), jnp.bfloat16),
             pltpu.SemaphoreType.DMA((1 + n_tiles,)),
+            pltpu.SemaphoreType.DMA,
             pltpu.SemaphoreType.DMA((len(AMP_STEPS),)),
             pltpu.SemaphoreType.DMA((len(AMP_STEPS),)),
             pltpu.SemaphoreType.DMA((len(GROUPS), len(INT_STEPS))),
@@ -416,24 +431,20 @@
         ],
         name="ladder",
         compiler_params=pltpu.CompilerParams(
-            collective_id=0, has_side_effects=True, vmem_limit_bytes=56 * 1024 * 1024
+            collective_id=0, has_side_effects=True, vmem_limit_bytes=111 * 512 * 1024
         ),
     )(
-        send_tiles, positions, amp_mask, pair_dest.reshape(1, pair_rows), amplitudes,
+        int_tiles.reshape(n_rows, slots), amp_mask.T, pair_dest.reshape(1, pair_rows), amplitudes,
         integrals.reshape(k_tiles, TILE, int_cols),
     )
-    parts_out = 8
     return pl.pallas_call(
         copy_kernel,
         out_shape=jax.ShapeDtypeStruct(spread.shape, spread.dtype),
-        in_specs=[any_ref],
+        in_specs=[vmem],
         out_specs=any_ref,
-        scratch_shapes=[
-            pltpu.VMEM((parts_out, CAP, n_cols * int_cols // parts_out), jnp.bfloat16),
-            pltpu.SemaphoreType.DMA((parts_out,)),
-            pltpu.SemaphoreType.DMA((parts_out,)),
-        ],
+        scratch_shapes=[pltpu.SemaphoreType.DMA((8,))],
         name="deliver",
+        compiler_params=pltpu.CompilerParams(vmem_limit_bytes=4 * 1024 * 1024),
     )(spread)
 
 

time: 163 us -> 157 us (0.963)
  local copies, waits for them, and re-layouts: 2.04 us -> 0 us
  Pallas kernels: 157 us -> 155 us
  other arithmetic: 1.69 us -> 0 us
    pallas_call x1, Pallas kernels: 6.42 us -> 3.37 us  [on_device(): pl.pallas_call(copy_kernel, out_shape=jax.ShapeDtypeStruct(spread.shape,...]
where the time goes in v3:
time: 157 us; the launch traced here: 155 us
  Pallas kernels  155 us (99%)
    pallas_call x1, Pallas kernels, on_device(): pl.pallas_call(ladder_kernel, out_shape=pltpu.VMEM((CAP, n_cols * int_col...  152 us
    pallas_call x1, Pallas kernels, on_device(): pl.pallas_call(copy_kernel, out_shape=jax.ShapeDtypeStruct(spread.shape,...  3.37 us

profile of v3, /device:TPU:1, one launch (start us, length us, event | category | flops | bytes accessed | tf_op | source)
XLA Modules:
  0.0 155.0 jit_solution(11242922289303032397)
XLA Ops:
  0.0 151.6 %ladder.1.src = bf16[128,32768]{1,0:T(8,128)(2,1)S(1)} custom-call(s32[8,32]{1,0:T(8,128)} %bitcast.5, s32[2,8]{1,0:T(2,128)} %bitcast.7, s32[1,1024]{1,0:T(1,128)} %bitcast.6, bf16[1024,256]{1,0:T(8,128)(2,1)} %amp_hbm.1, bf16[4,128,2048]{2,1,0:T(8,128)(2,1)} %bitcast.4), custom_call_target="tpu_custom_call" | custom-call | tf_op jit(solution)/shard_map/ladder/pallas_call | solution.py:404
  151.6 3.4 %deliver.1 = bf16[128,32768]{1,0:T(8,128)(2,1)} custom-call(bf16[128,32768]{1,0:T(8,128)(2,1)S(1)} %ladder.1.src), custom_call_target="tpu_custom_call" | custom-call | tf_op jit(solution)/shard_map/deliver/pallas_call | solution.py:440

commit v4 on v3

--- a/solution.py
+++ b/solution.py
@@ -13,7 +13,8 @@
 CHUNK_TILES = 2
 CHUNK = CHUNK_TILES * TILE
 GROUPS = (8, 8, 8, 8)
-PART = 4
+PART = 2
+FIRST_STEP = 10
 
 AMP_STEPS = {
     "x0": ((0, 0, 0), 0, (1, 0, 0)),
@@ -199,8 +200,9 @@
         earlier = jnp.where(q < p, 1.0, 0.0).astype(jnp.bfloat16)
         before = jnp.dot(onehot.astype(jnp.bfloat16), earlier, preferred_element_type=jnp.float32)
         slot = jnp.sum(before * onehot[:, cols], axis=0, keepdims=True)
-        ahead = pair_dest[:, cols] - col
-        key[:, cols] = jnp.where(ahead < 0, ahead + n_cols, ahead) * CAP + slot.astype(jnp.int32)
+        ahead = pair_dest[:, cols] - col - FIRST_STEP + n_cols
+        ahead = jnp.where(ahead < 0, ahead + n_cols, ahead)
+        key[:, cols] = jnp.where(ahead >= n_cols, ahead - n_cols, ahead) * CAP + slot.astype(jnp.int32)
 
     def fill_select(d, carry):
         places = lax.broadcasted_iota(jnp.int32, (CAP, pair_rows), 0) + d * CAP
@@ -245,23 +247,25 @@
     def out_piece(owner, q):
         return out.at[:, pl.ds(pl.multiple_of(owner * int_cols + q * CHUNK, CHUNK), CHUNK)]
 
+    n_parts = n_cols // PART
+    own_place_at = n_cols - FIRST_STEP
+
     def send_part(q, j):
-        for i in range(PART):
-            step = j * PART + i
+        for place in range(j * PART, (j + 1) * PART):
+            step = (place + FIRST_STEP) % n_cols
             peer = lax.rem(col + step, n_cols)
 
             def to_peer():
                 pltpu.make_async_remote_copy(
-                    stage.at[q, step], out_piece(col, q), out_send.at[step], out_recv.at[step],
+                    stage.at[q, place], out_piece(col, q), out_send.at[step], out_recv.at[step],
                     device_id=(row, peer), device_id_type=MESH,
                 ).start()
 
             if step == 0:
-                pltpu.make_async_copy(stage.at[q, 0], out_piece(col, q), own_sem.at[q]).start()
+                pltpu.make_async_copy(stage.at[q, own_place_at], out_piece(col, q), own_sem.at[q]).start()
             else:
                 to_peer()
 
-    n_parts = n_cols // PART
 
     def spread(q):
         for j in range(n_parts):
@@ -323,6 +327,8 @@
     amp_start("cxq1")
     int_arrived(1, "xp", "xm")
     int_start(1, "xpp", "xmm")
+    int_arrived(2, "x")
+    int_start(2, "xp", "xm")
     amp_arrived("cxp")
     multiply(far + lax.rem(y + 3, 4) * y_cols, y_cols, False, False)
     amp_arrived("cxm")
@@ -331,8 +337,6 @@
     multiply(far + lax.rem(y + 2, 4) * y_cols, y_cols, False, True)
     spread(0)
 
-    int_arrived(2, "x")
-    int_start(2, "xp", "xm")
     int_arrived(2, "p", "m")
     int_start(2, "pp", "mm")
     int_start(3, "p", "m")
@@ -359,7 +363,7 @@
             int_copy(g, name, False).wait_send()
 
     def own_done(q, carry):
-        pltpu.make_async_copy(stage.at[q, 0], out_piece(col, q), own_sem.at[q]).wait()
+        pltpu.make_async_copy(stage.at[q, own_place_at], out_piece(col, q), own_sem.at[q]).wait()
         return carry
 
     lax.fori_loop(0, n_chunks, own_done, 0)

time: 157 us -> 149 us (0.949); the launches traced: 155 us -> 149 us
  Pallas kernels: 155 us -> 149 us
    pallas_call x1, Pallas kernels: 152 us -> 146 us  [on_device(): pl.pallas_call(ladder_kernel, out_shape=pltpu.VMEM((CAP, n_cols * int_col...]
where the time goes in v4:
time: 149 us
  Pallas kernels  149 us (100%)
    pallas_call x1, Pallas kernels, on_device(): pl.pallas_call(ladder_kernel, out_shape=pltpu.VMEM((CAP, n_cols * int_col...  146 us
    pallas_call x1, Pallas kernels, on_device(): pl.pallas_call(copy_kernel, out_shape=jax.ShapeDtypeStruct(spread.shape,...  3.37 us

profile of v4, /device:TPU:1, one launch (start us, length us, event | category | flops | bytes accessed | tf_op | source)
XLA Modules:
  0.0 149.2 jit_solution(1061866511925569325)
XLA Ops:
  0.0 145.9 %ladder.1.src = bf16[128,32768]{1,0:T(8,128)(2,1)S(1)} custom-call(s32[8,32]{1,0:T(8,128)} %bitcast.5, s32[2,8]{1,0:T(2,128)} %bitcast.7, s32[1,1024]{1,0:T(1,128)} %bitcast.6, bf16[1024,256]{1,0:T(8,128)(2,1)} %amp_hbm.1, bf16[4,128,2048]{2,1,0:T(8,128)(2,1)} %bitcast.4), custom_call_target="tpu_custom_call" | custom-call | tf_op jit(solution)/shard_map/ladder/pallas_call | solution.py:408
  145.9 3.4 %deliver.1 = bf16[128,32768]{1,0:T(8,128)(2,1)} custom-call(bf16[128,32768]{1,0:T(8,128)(2,1)S(1)} %ladder.1.src), custom_call_target="tpu_custom_call" | custom-call | tf_op jit(solution)/shard_map/deliver/pallas_call | solution.py:444

commit v5 on v4

--- a/solution.py
+++ b/solution.py
@@ -14,7 +14,7 @@
 CHUNK = CHUNK_TILES * TILE
 GROUPS = (8, 8, 8, 8)
 PART = 2
-FIRST_STEP = 10
+FIRST_STEP = 9
 
 AMP_STEPS = {
     "x0": ((0, 0, 0), 0, (1, 0, 0)),
@@ -446,7 +446,7 @@
         out_shape=jax.ShapeDtypeStruct(spread.shape, spread.dtype),
         in_specs=[vmem],
         out_specs=any_ref,
-        scratch_shapes=[pltpu.SemaphoreType.DMA((8,))],
+        scratch_shapes=[pltpu.SemaphoreType.DMA((4,))],
         name="deliver",
         compiler_params=pltpu.CompilerParams(vmem_limit_bytes=4 * 1024 * 1024),
     )(spread)

time: 149 us -> 149 us (level)
  no operation moved by 1% of the time
where the time goes in v5:
time: 149 us
  Pallas kernels  149 us (100%)
    pallas_call x1, Pallas kernels, on_device(): pl.pallas_call(ladder_kernel, out_shape=pltpu.VMEM((CAP, n_cols * int_col...  145 us
    pallas_call x1, Pallas kernels, on_device(): pl.pallas_call(copy_kernel, out_shape=jax.ShapeDtypeStruct(spread.shape,...  3.37 us

profile of v5, /device:TPU:1, one launch (start us, length us, event | category | flops | bytes accessed | tf_op | source)
XLA Modules:
  0.0 148.7 jit_solution(9013995571397068428)
XLA Ops:
  0.0 145.3 %ladder.1.src = bf16[128,32768]{1,0:T(8,128)(2,1)S(1)} custom-call(s32[8,32]{1,0:T(8,128)} %bitcast.5, s32[2,8]{1,0:T(2,128)} %bitcast.7, s32[1,1024]{1,0:T(1,128)} %bitcast.6, bf16[1024,256]{1,0:T(8,128)(2,1)} %amp_hbm.1, bf16[4,128,2048]{2,1,0:T(8,128)(2,1)} %bitcast.4), custom_call_target="tpu_custom_call" | custom-call | tf_op jit(solution)/shard_map/ladder/pallas_call | solution.py:408
  145.3 3.4 %deliver.1 = bf16[128,32768]{1,0:T(8,128)(2,1)} custom-call(bf16[128,32768]{1,0:T(8,128)(2,1)S(1)} %ladder.1.src), custom_call_target="tpu_custom_call" | custom-call | tf_op jit(solution)/shard_map/deliver/pallas_call | solution.py:444
